TPU v7x, 256 devices: a whole 4x4x8 slice. The times are simulated.
256 devices in a mesh: ctx: 64 (over x, z, core), tp: 4 (over y).
Axes of the slice: x: 4, y: 4, z: 8, core: 2. Of those that a mesh axis runs over, the one named last changes fastest.
Arguments:
- query: bfloat16 [32768, 4096], P('ctx', 'tp'), may hold values from -6 to 6
- key_in: bfloat16 [32768, 4096], P('ctx', 'tp'), may hold values from -6 to 6
- value: bfloat16 [32768, 4096], P('ctx', 'tp'), may hold values from -6 to 6
- rates: float32 [256, 16], P('tp'), as said below
- residues: float32 [256, 16], P('tp'), as said below
- skip_gain: float32 [4096], P('tp'), may hold values from 0.5 to 1.5
- out_weight: bfloat16 [4096, 4096], P('tp'), may hold values from -0.09375 to 0.09375
Outputs:
- layer_out: bfloat16 [32768, 4096], P('ctx', 'tp')
Inputs may be any that keep to these rules, and one draw needn't show every extreme that they name: `rates`: positive, at most 0.0625. `residues`: either sign.
All inputs are finite; a program needn't handle non-finite values.
Results may differ from a plain program's by a relative error of at most 0.0095.
Values may be sent and summed in bfloat16 or wider, within the bound.
A program may use at most 128 MiB of HBM per device.

v0:
```python
import jax
import jax.numpy as jnp
from jax import lax
from jax.sharding import PartitionSpec as P

GROUP = 16
SUB = 128


def shards(query, key_in, value, rates, residues, skip_gain, out_weight):
    tok_rows, channels = query.shape
    groups_here = channels // GROUP
    sub_count = tok_rows // SUB
    product_bf = (key_in.astype(jnp.float32) * value.astype(jnp.float32)).astype(jnp.bfloat16)
    signal = product_bf.astype(jnp.float32).T
    positions = jnp.arange(SUB, dtype=jnp.float32)
    filter_local = jnp.sum(
        residues[:, :, None] * jnp.exp(-rates[:, :, None] * positions[None, None, :]), axis=1
    )
    lag_index = (
        jnp.arange(SUB, dtype=jnp.int32)[:, None] - jnp.arange(SUB, dtype=jnp.int32)[None, :]
    )
    toeplitz = jnp.where(
        lag_index[None] >= 0, jnp.take(filter_local, jnp.clip(lag_index, 0, SUB - 1), axis=1), 0.0
    )
    grouped = (
        signal.reshape(groups_here, GROUP, sub_count, SUB)
        .transpose(0, 3, 1, 2)
        .reshape(groups_here, SUB, GROUP * sub_count)
    )
    local = jnp.einsum("gts,gsn->gtn", toeplitz, grouped, precision=lax.Precision.HIGHEST)
    local = (
        local.reshape(groups_here, SUB, GROUP, sub_count)
        .transpose(0, 2, 3, 1)
        .reshape(channels, tok_rows)
    )
    rate_cols = jnp.repeat(rates, GROUP, axis=0).T
    residue_cols = jnp.repeat(residues, GROUP, axis=0).T
    decay_in = jnp.exp(-rate_cols[:, :, None] * (SUB - 1.0 - positions)[None, None, :])
    sub_sums = jnp.einsum(
        "mcs,cjs->mcj",
        decay_in,
        signal.reshape(channels, sub_count, SUB),
        precision=lax.Precision.HIGHEST,
    )
    sub_decay = jnp.exp(-rate_cols * SUB)
    inner = [jnp.zeros_like(rate_cols)]
    for index_sub in range(sub_count):
        inner.append(sub_decay * inner[-1] + sub_sums[:, :, index_sub])
    summary = inner[sub_count]
    block_index = lax.axis_index("ctx")
    piece = lax.all_gather(summary[None], "ctx", axis=0, tiled=True)
    count = piece.shape[0]
    distance = block_index - 1 - jnp.arange(count, dtype=jnp.int32)
    spans = (tok_rows * jnp.maximum(distance, 0)).astype(jnp.float32)
    weight = jnp.where(
        distance[:, None, None] >= 0, jnp.exp(-rate_cols[None] * spans[:, None, None]), 0.0
    )
    state = jnp.sum(weight * piece, axis=0)
    starts = [
        inner[index_sub] + jnp.exp(-rate_cols * (SUB * index_sub * 1.0)) * state
        for index_sub in range(sub_count)
    ]
    start_states = jnp.stack(starts, axis=2)
    decay_out = residue_cols[:, :, None] * jnp.exp(
        -rate_cols[:, :, None] * (positions + 1.0)[None, None, :]
    )
    past = jnp.einsum(
        "mct,mcj->cjt", decay_out, start_states, precision=lax.Precision.HIGHEST
    ).reshape(channels, tok_rows)
    conv = local + past
    mixed = (query.astype(jnp.float32).T * (conv + skip_gain[:, None] * signal)).astype(
        jnp.bfloat16
    )
    summed = lax.psum_scatter(
        lax.dot_general(
            out_weight, mixed, (((0,), (0,)), ((), ())), preferred_element_type=jnp.float32
        ),
        "tp",
        scatter_dimension=0,
        tiled=True,
    )
    return summed.T.astype(jnp.bfloat16)


def solution(mesh):
    in_specs = (
        P("ctx", "tp"),
        P("ctx", "tp"),
        P("ctx", "tp"),
        P("tp", None),
        P("tp", None),
        P("tp"),
        P("tp", None),
    )
    out_specs = P("ctx", "tp")
    return jax.shard_map(shards, mesh=mesh, in_specs=in_specs, out_specs=out_specs, check_vma=False)
```

profile of v0, /device:TPU:1, one launch (start us, length us, event | category | flops | bytes accessed | tf_op | source)
XLA Modules:
  0.0 222.6 jit_solution(9311980342406454781)
XLA Ops:
  6.5 0.8 neg.21
  7.5 0.3 neg.22
  7.8 1.0 copy.94
  8.8 1.5 copy.92
  10.3 0.5 copy.93
  10.9 0.3 fusion.25
  11.2 1.1 reshape.111
  12.3 9.6 %fusion.4 = f32[1024,4,16]{2,1,0:T(4,128)} fusion(bf16[1024,4,128]{2,1,0:T(4,128)(2,1)} %reshape.111, f32[128]{0:T(128)S(1)} %iota_subtract_fusion.1, f32[16,1024]{0,1:T(8,128)} %copy.94), kind=kOutput, calls=%fused_computation.5 | convolution fusion | flops 102760448 | bytes 1376768 | tf_op jit(solution)/shard_map/mcs,cjs->mcj/dot_general | solution.py:40
  21.9 1.8 copy.95
  23.8 0.7 fusion.28
  24.5 0.2 reduce-scatter.2.cloned.1.call-start
  24.7 1.1 reshape.107
  26.0 0.3 multiply_reduce_fusion.1
  26.5 54.4 %gather_fusion = f32[16384,64]{1,0:T(8,128)} fusion(f32[64,128]{0,1:T(8,128)S(1)} %copy.90, s32[16384]{0:T(1024)S(1)} %fusion.27), kind=kCustom, calls=%fused_computation | custom fusion | bytes 8454144 | tf_op jit(solution)/shard_map/jit(_take)/gather | solution.py:24
  80.9 7.3 %copy.91 = f32[128,128,64]{1,0,2:T(8,128)} copy(f32[128,128,64]{2,1,0:T(8,128)} %bitcast.109) | data formatting | bytes 8388608 | tf_op jit(solution)/shard_map/jit(_take)/gather | solution.py:24
  88.2 1.5 copy.87
  89.8 8.2 %fusion.7 = f32[64,128,64]{1,2,0:T(8,128)} fusion(bf16[64,128,64]{1,2,0:T(8,128)(2,1)} %bitcast.113, f32[128,128,64]{1,0,2:T(8,128)} %copy.91, pred[128,128]{1,0:T(8,128)(4,1)S(1)} %get-tuple-element.9, pred[128,128]{1,0:T(8,128)(4,1)S(1)} %get-tuple-element.10), kind=kOutput, calls=%fused_computation.9 | convolution fusion | flops 807403520 | bytes 7372800 | tf_op jit(solution)/shard_map/gts,gsn->gtn/dot_general | solution.py:31
  98.0 9.8 %all-gather.3.cloned.1.call-done = f32[1024,1024]{1,0:T(8,128)} async-done(((f32[16,1024]{1,0:T(8,128)}), f32[1024,1024]{1,0:T(8,128)}) %all-gather.3.cloned.1.call-update) | async-done | bytes 4194320 | tf_op jit(solution)/shard_map/all_gather | solution.py:52
  107.8 3.1 %multiply_reduce_fusion = f32[16,1024]{1,0:T(8,128)S(1)} fusion(f32[64,16,1024]{2,1,0:T(8,128)} %bitcast.114, f32[64]{0:T(128)S(1)} %multiply_convert_fusion.2, f32[16,1024]{1,0:T(8,128)S(1)} %bitcast.119, pred[64]{0:T(512)(128)(4,1)S(1)} %fusion.36), kind=kLoop, calls=%fused_computation.15 | loop fusion | flops 4177920 | bytes 4325696 | tf_op jit(solution)/shard_map/reduce_sum | solution.py:59
  111.0 1.7 copy.97
  112.8 12.3 %fusion = f32[1024,4,128]{2,1,0:T(4,128)S(1)} fusion(f32[16,1024,4]{0,2,1:T(4,128)} %copy.97, f32[128]{0:T(128)S(1)} %iota_add_fusion, f32[16,1024]{0,1:T(8,128)S(1)} %bitcast.120, f32[16,1024]{0,1:T(8,128)} %copy.94), kind=kOutput, calls=%fused_computation.1 | convolution fusion | flops 104857600 | bytes 2490880 | tf_op jit(solution)/shard_map/mct,mcj->cjt/dot_general | solution.py:68
  125.2 7.8 %convolution_bitcast_fusion = f32[4096,512]{0,1:T(8,128)} fusion(bf16[1024,4096]{1,0:T(8,128)(2,1)S(1)} %bitcast.111, f32[128,8,4,128]{3,2,1,0:T(4,128)S(1)} %bitcast.115, f32[128,8,4,128]{3,2,1,0:T(4,128)S(1)} %bitcast.112, bf16[512,1024]{0,1:T(8,128)(2,1)S(1)} %copy.87, f32[1024]{0:T(1024)S(1)} %copy-done.2, bf16[512,1024]{0,1:T(8,128)(2,1)S(1)} %copy.93, ...), kind=kOutput, calls=%fused_computation.8 | convolution fusion | flops 4300734464 | bytes 24121344 | tf_op jit(solution)/shard_map/dot_general | solution.py:76
  133.1 80.0 %reduce-scatter.2.cloned.1.call-done = f32[1024,512]{0,1:T(8,128)} async-done(((f32[4096,512]{0,1:T(8,128)}), f32[1024,512]{0,1:T(8,128)}) %reduce-scatter.2.cloned.1.call-update) | async-done | bytes 2097168 | tf_op jit(solution)/shard_map/reduce_scatter | solution.py:75
  213.1 2.7 %convert_bitcast_fusion = bf16[512,1024]{1,0:T(8,128)(2,1)} fusion(f32[1024,512]{0,1:T(8,128)} %reduce-scatter.2.cloned.1.call-done), kind=kLoop, calls=%fused_computation.28 | loop fusion | flops 524288 | bytes 3145728 | tf_op jit(solution)/shard_map/convert_element_type | solution.py:83
  (29 shorter events, 0.7 us)
Async XLA Ops:
  6.5 3.8 %copy-start.1 = (bf16[512,1024]{1,0:T(8,128)(2,1)S(1)}, bf16[512,1024]{1,0:T(8,128)(2,1)}, u32[]{:S(2)}) copy-start(bf16[512,1024]{1,0:T(8,128)(2,1)} %param.9) | copy-start | bytes 3145732
  6.5 101.3 %all-gather.3.cloned.1.call-start = ((), (), s32[]{:S(2)}) async-start(), calls=%async_computation.2 | async-start | bytes 4259840 | tf_op jit(solution)/shard_map/all_gather | solution.py:52
  21.9 4.0 %copy-start.3 = (f32[64,16]{0,1:T(8,128)S(1)}, f32[64,16]{0,1:T(8,128)}, u32[]{:S(2)}) copy-start(f32[64,16]{0,1:T(8,128)} %param.11) | copy-start | bytes 12292
  24.5 188.6 %reduce-scatter.2.cloned.1.call-start = ((), (), s32[]{:S(2)}) async-start(), calls=%async_computation.1 | async-start | bytes 10485760 | tf_op jit(solution)/shard_map/reduce_scatter | solution.py:75
  112.8 12.4 %slice-start = ((s8[8388608]{0:T(1024)(128)(4,1)}), s8[4194304]{0:T(1024)(128)(4,1)S(1)}, s32[]{:S(2)}) async-start(s8[8388608]{0:T(1024)(128)(4,1)} %bitcast.110), calls=%async_computation.3 | async-start | bytes 8388608
  112.8 12.4 %slice-start.1 = ((s8[8388608]{0:T(1024)(128)(4,1)}), s8[4194304]{0:T(1024)(128)(4,1)S(1)}, s32[]{:S(2)}) async-start(s8[8388608]{0:T(1024)(128)(4,1)} %bitcast.110), calls=%async_computation.4 | async-start | bytes 8388608
  112.8 12.4 %copy-start = (f32[64,128,64]{1,2,0:T(8,128)S(1)}, f32[64,128,64]{1,2,0:T(8,128)}, u32[]{:S(2)}) copy-start(f32[64,128,64]{1,2,0:T(8,128)} %fusion.7) | copy-start | bytes 6291460
  112.8 12.4 %copy-start.2 = (f32[1024]{0:T(1024)S(1)}, f32[1024]{0:T(1024)}, u32[]{:S(2)}) copy-start(f32[1024]{0:T(1024)} %param.12) | copy-start | bytes 12292
Sparse Core Ops, SparseCore 0:
  24.6 83.1 all-gather.2
  133.2 79.8 reduce-scatter.1
where the time goes:
time: 223 us
  waiting for transfers between devices  89.8 us (40%)
  local copies, waits for them, and re-layouts  72.9 us (33%)
  matrix products  38 us (17%)
  between operations  13.6 us (6%)
  other arithmetic  8.14 us (4%)
    reduce_scatter x1, waiting for transfers between devices, shards(): lax.psum_scatter(lax.dot_general(out_weight, mixed, (((0,), (0,)), ((), (...  80 us
    gather x2, local copies, waits for them, and re-layouts, shards(): jnp.take(filter_local, jnp.clip(lag_index, 0, SUB - 1), axis=1)  61.8 us
    dot_general x1, matrix products, shards(): jnp.einsum('mct,mcj->cjt', decay_out, start_states, precision=lax.Precisi...  12.3 us
    all_gather x1, waiting for transfers between devices, shards(): piece = lax.all_gather(summary[None], 'ctx', axis=0, tiled=True)  9.76 us
    dot_general x1, matrix products, shards(): jnp.einsum('mcs,cjs->mcj', decay_in, signal.reshape(channels, sub_count,...  9.63 us
    dot_general x1, matrix products, shards(): jnp.einsum('gts,gsn->gtn', toeplitz, grouped, precision=lax.Precision.HIG...  8.22 us
    dot_general x1, matrix products, shards(): lax.dot_general(out_weight, mixed, (((0,), (0,)), ((), ())), preferred_el...  7.85 us
  transfers between devices with their start and end apart: 2, of which 2 were waited for; matrix products, arithmetic and copies ran while one was open for 33% of the time, Pallas kernels for 0%

commit v1 on v0

v1 whole, which is shorter than its diff:
```python
import functools

import jax
import jax.numpy as jnp
from jax import lax
from jax.experimental import pallas as pl
from jax.experimental.pallas import tpu as pltpu
from jax.sharding import PartitionSpec as P

GROUP = 16
MODES = 16
SUB = 128
LANES = 128
BLK = 256
MESH = pl.DeviceIdType.MESH
F32 = jnp.float32
BF16 = jnp.bfloat16


def dot(a, b):
    return jnp.dot(a, b, preferred_element_type=F32)


def split(a):
    high = a.astype(BF16)
    return high, (a - high.astype(F32)).astype(BF16)


def kernel(
    lines,
    q_hbm,
    k_hbm,
    v_hbm,
    w_hbm,
    rates_ref,
    residues_ref,
    skip_ref,
    o_hbm,
    qb,
    kb,
    vb,
    ub,
    wb,
    ob,
    mixed,
    local,
    d_tab,
    a_hi,
    a_lo,
    h_pad,
    toep,
    sums,
    rate3,
    s_send,
    s_recv,
    l_send,
    l_recv,
    x_send,
    x_recv,
    far_s,
    far_r,
    near_s,
    near_r,
    lsem,
    osem,
    s_ss,
    s_rs,
    l_ss,
    l_rs,
    x_ss,
    x_rs,
    far_ss,
    far_rs,
    near_ss,
    near_rs,
):
    rows, chans = ub.shape
    subs = rows // SUB
    groups = chans // GROUP
    blocks = chans // BLK
    half = chans // 2
    per_line = s_send.shape[0]
    own = s_send.shape[1]

    ctx, tp = lax.axis_index("ctx"), lax.axis_index("tp")
    mx, mj = lax.div(ctx, per_line), lax.rem(ctx, per_line)
    right, left = lax.rem(tp + 1, 4), lax.rem(tp + 3, 4)
    sides = ((ctx, right), (ctx, left))

    def peer_j(k):
        return lax.rem(mj + k, per_line)

    def peer_x(k):
        return lax.rem(mx + k, lines)

    barrier = pltpu.get_barrier_semaphore()
    for k in range(1, per_line):
        pl.semaphore_signal(
            barrier, inc=1, device_id=(mx * per_line + peer_j(k), tp), device_id_type=MESH
        )
    for k in range(1, lines):
        pl.semaphore_signal(
            barrier, inc=1, device_id=(peer_x(k) * per_line + mj, tp), device_id_type=MESH
        )
    for side in sides:
        pl.semaphore_signal(barrier, inc=1, device_id=side, device_id_type=MESH)

    loads = [
        pltpu.make_async_copy(k_hbm, kb, lsem.at[0]),
        pltpu.make_async_copy(v_hbm, vb, lsem.at[1]),
        pltpu.make_async_copy(q_hbm, qb, lsem.at[2]),
    ]
    w_loads = {}
    for r in (2, 1, 3, 0):
        start = pl.multiple_of(lax.rem(tp + r, 4) * chans, chans)
        w_loads[r] = pltpu.make_async_copy(
            w_hbm.at[:, pl.ds(start, chans)], wb.at[r], lsem.at[3 + r]
        )
    for load in loads:
        load.start()
    for load in w_loads.values():
        load.start()

    rates, residues = rates_ref[...].T, residues_ref[...].T
    pick = lax.broadcasted_iota(jnp.int32, (chans, MODES), 1) == (
        lax.broadcasted_iota(jnp.int32, (chans, MODES), 0) & (MODES - 1)
    )

    def column(a):
        spread = jnp.broadcast_to(a[:, None, :], (groups, MODES, MODES)).reshape(chans, MODES)
        return jnp.sum(jnp.where(pick, spread, 0.0), axis=1, keepdims=True)

    rate_col, residue_col = column(rates), column(residues)
    lag = lax.broadcasted_iota(jnp.int32, (chans, SUB), 1).astype(F32)
    decay_in = jnp.exp(-rate_col * (SUB - 1.0 - lag))
    high, low = split(decay_in)
    d_tab[:, :SUB] = high
    d_tab[:, SUB:] = low
    spread = (
        lax.shift_right_logical(lax.broadcasted_iota(jnp.int32, (groups, chans), 1), 4)
        == lax.broadcasted_iota(jnp.int32, (groups, chans), 0)
    ).astype(F32)
    rate_row = jnp.dot(
        rates_ref[...], spread, precision=lax.Precision.HIGHEST, preferred_element_type=F32
    )
    for k in range(chans // LANES):
        rate3[:, k, :] = rate_row[:, k * LANES : (k + 1) * LANES]
    same_group = lax.shift_right_logical(
        lax.broadcasted_iota(jnp.int32, (BLK, BLK), 0), 4
    ) == lax.shift_right_logical(lax.broadcasted_iota(jnp.int32, (BLK, BLK), 1), 4)
    diag = same_group.astype(F32)

    loads[0].wait()
    loads[1].wait()
    for j in range(subs):
        at = pl.ds(j * SUB, SUB)
        for b in range(blocks):
            cols = pl.ds(b * BLK, BLK)
            u = (kb[at, cols].astype(F32) * vb[at, cols].astype(F32)).astype(BF16)
            ub[at, cols] = u
            full = dot(d_tab[cols, :], jnp.concatenate([u, u], axis=0))
            sums[j, :, cols] = jnp.sum((full * diag).reshape(BLK // MODES, MODES, BLK), axis=0)
    step_decay = jnp.exp(-rate_row * SUB)
    state = jnp.zeros_like(rate_row)
    for j in range(subs):
        following = step_decay * state + sums[j]
        sums[j] = state
        state = following
    for k in range(chans // LANES):
        piece = state[:, k * LANES : (k + 1) * LANES]
        s_send[:, :, k, :] = piece.reshape(per_line, own, LANES)

    pl.semaphore_wait(barrier, per_line - 1 + lines - 1 + 2)

    def s_copy(k):
        to = peer_j(k)
        return pltpu.make_async_remote_copy(
            src_ref=s_send.at[to],
            dst_ref=s_recv.at[mj],
            send_sem=s_ss.at[k],
            recv_sem=s_rs.at[k],
            device_id=(mx * per_line + to, tp),
            device_id_type=MESH,
        )

    def l_copy(k):
        return pltpu.make_async_remote_copy(
            src_ref=l_send,
            dst_ref=l_recv.at[mx],
            send_sem=l_ss.at[k],
            recv_sem=l_rs.at[k],
            device_id=(peer_x(k) * per_line + mj, tp),
            device_id_type=MESH,
        )

    def x_copy(k):
        to = peer_j(k)
        return pltpu.make_async_remote_copy(
            src_ref=x_send.at[to],
            dst_ref=x_recv.at[mj],
            send_sem=x_ss.at[k],
            recv_sem=x_rs.at[k],
            device_id=(mx * per_line + to, tp),
            device_id_type=MESH,
        )

    for k in range(1, per_line):
        s_copy(k).start()
    s_recv[mj] = s_send[mj]

    taps = jnp.sum((decay_in * residue_col).reshape(groups, MODES, SUB), axis=1)
    h_pad[:, :SUB] = taps
    h_pad[:, SUB:] = jnp.zeros_like(taps)

    def build(n, carry):
        for side in range(2):
            row = jnp.broadcast_to(h_pad[pl.ds(2 * n + side, 1), :], (SUB, 2 * SUB))
            turned = pltpu.roll(row, SUB + 1, 1, stride=1, stride_axis=0)
            toep[n, :, side * SUB : (side + 1) * SUB] = turned[:, :SUB].astype(BF16)
        return carry

    lax.fori_loop(0, groups // 2, build, 0)

    for k in range(1, per_line):
        s_copy(k).wait_recv()
    my_rate = rate3[pl.ds(mj * own, own)]
    block_decay = jnp.exp(-my_rate * rows)
    total = jnp.zeros_like(my_rate)
    for j in range(per_line):
        x_send[j] = total
        total = block_decay * total + s_recv[j]
    l_send[...] = total
    for k in range(1, lines):
        l_copy(k).start()

    def inside(n, carry):
        j, b = lax.div(n, blocks), lax.rem(n, blocks)
        at = pl.ds(pl.multiple_of(j * SUB, SUB), SUB)
        cols = pl.ds(pl.multiple_of(b * BLK, BLK), BLK)
        u = ub[at, cols]
        acc = skip_ref[:, cols] * u.astype(F32)
        lane_group = lax.shift_right_logical(lax.broadcasted_iota(jnp.int32, (1, BLK), 1), 4)
        for pair in range(BLK // GROUP // 2):
            masked = [
                u * (lane_group == 2 * pair + side).astype(F32).astype(BF16) for side in range(2)
            ]
            acc += dot(toep[b * (BLK // GROUP // 2) + pair], jnp.concatenate(masked, axis=0))
        local[at, cols] = acc
        return carry

    first_part = subs * blocks // 2
    lax.fori_loop(0, first_part, inside, 0)

    for k in range(1, lines):
        l_copy(k).wait_recv()
    entering = jnp.zeros_like(total)
    for other in range(lines):
        distance = mx - 1 - other
        weight = jnp.exp(-my_rate * (jnp.maximum(distance, 0) * (per_line * rows)).astype(F32))
        entering += jnp.where(distance >= 0, weight * l_recv[other], 0.0)
    for j in range(per_line):
        x_send[j] = x_send[j] + entering
        entering = entering * block_decay
    for k in range(1, per_line):
        x_copy(k).start()
    x_recv[mj] = x_send[mj]

    high, low = split((residue_col * jnp.exp(-rate_col * (lag + 1.0))).T)
    a_hi[...] = high
    a_lo[...] = low
    lax.fori_loop(first_part, subs * blocks, inside, 0)
    loads[2].wait()
    for k in range(1, per_line):
        x_copy(k).wait_recv()

    def far_copy(way, j):
        return pltpu.make_async_remote_copy(
            src_ref=far_s.at[way, j],
            dst_ref=far_r.at[way, j],
            send_sem=far_ss.at[way, j],
            recv_sem=far_rs.at[way, j],
            device_id=sides[way],
            device_id_type=MESH,
        )

    def near_copy(way, part, j):
        return pltpu.make_async_remote_copy(
            src_ref=near_s.at[way, part, j],
            dst_ref=near_r.at[way, part, j],
            send_sem=near_ss.at[way, part, j],
            recv_sem=near_rs.at[way, part, j],
            device_id=sides[way],
            device_id_type=MESH,
        )

    def project(j, r, part):
        at = pl.ds(pl.multiple_of(j * SUB, SUB), SUB)
        return dot(mixed[at, :], wb[r, :, part * half : (part + 1) * half])

    w_loads[2].wait()
    entry = jnp.concatenate(
        [x_recv[:, :, k, :].reshape(MODES, LANES) for k in range(chans // LANES)], axis=1
    )
    diag_bf = diag.astype(BF16)

    def far_step(j, carry):
        at = pl.ds(pl.multiple_of(j * SUB, SUB), SUB)
        start = jnp.exp(-rate_row * (j * SUB).astype(F32)) * entry + sums[j]
        x_hi, x_lo = split(start)
        for b in range(blocks):
            cols = slice(b * BLK, (b + 1) * BLK)
            wide_hi = jnp.concatenate([x_hi[:, cols]] * (BLK // MODES), axis=0) * diag_bf
            wide_lo = jnp.concatenate([x_lo[:, cols]] * (BLK // MODES), axis=0) * diag_bf
            past = dot(a_hi[:, cols], wide_hi) + dot(a_lo[:, cols], wide_hi)
            past += dot(a_hi[:, cols], wide_lo)
            mixed[at, cols] = (qb[at, cols].astype(F32) * (local[at, cols] + past)).astype(BF16)
        for way in range(2):
            far_s[way, j] = project(j, 2, way).astype(BF16)
            far_copy(way, j).start()
        return carry

    lax.fori_loop(0, subs, far_step, 0)
    w_loads[1].wait()
    w_loads[3].wait()

    def direct_step(j, carry):
        for way in range(2):
            near_s[way, 1 - way, j] = project(j, 1 + 2 * way, 1 - way).astype(BF16)
            near_copy(way, 1 - way, j).start()
        return carry

    lax.fori_loop(0, subs, direct_step, 0)

    def joint_step(j, carry):
        for way in range(2):
            part = project(j, 1 + 2 * way, way)
            far_copy(way, j).wait_recv()
            near_s[way, way, j] = (part + far_r[way, j].astype(F32)).astype(BF16)
            near_copy(way, way, j).start()
        return carry

    lax.fori_loop(0, subs, joint_step, 0)
    w_loads[0].wait()

    def out_copy(j):
        at = pl.ds(pl.multiple_of(j * SUB, SUB), SUB)
        return pltpu.make_async_copy(ob.at[at], o_hbm.at[at], osem.at[j])

    def last_step(j, carry):
        at = pl.ds(pl.multiple_of(j * SUB, SUB), SUB)
        for part in range(2):
            mine = project(j, 0, part)
            near_copy(0, part, j).wait_recv()
            near_copy(1, part, j).wait_recv()
            mine += near_r[0, part, j].astype(F32) + near_r[1, part, j].astype(F32)
            ob[at, part * half : (part + 1) * half] = mine.astype(BF16)
        out_copy(j).start()
        return carry

    lax.fori_loop(0, subs, last_step, 0)

    def drain(j, carry):
        for way in range(2):
            far_copy(way, j).wait_send()
            for part in range(2):
                near_copy(way, part, j).wait_send()
        out_copy(j).wait()
        return carry

    lax.fori_loop(0, subs, drain, 0)
    for k in range(1, per_line):
        s_copy(k).wait_send()
        x_copy(k).wait_send()
    for k in range(1, lines):
        l_copy(k).wait_send()


def shards(lines, query, key_in, value, rates, residues, skip_gain, out_weight):
    rows, chans = query.shape
    groups = chans // GROUP
    subs = rows // SUB
    half = chans // 2
    per_line = lax.axis_size("ctx") // lines
    own = MODES // per_line
    tile = chans // LANES
    hbm = pl.BlockSpec(memory_space=pl.ANY)
    vmem = pl.BlockSpec(memory_space=pltpu.VMEM)
    dma = pltpu.SemaphoreType.DMA
    return pl.pallas_call(
        functools.partial(kernel, lines),
        name="hyena",
        out_shape=jax.ShapeDtypeStruct((rows, chans), BF16),
        in_specs=[hbm, hbm, hbm, hbm, vmem, vmem, vmem],
        out_specs=hbm,
        scratch_shapes=[
            pltpu.VMEM((rows, chans), BF16),
            pltpu.VMEM((rows, chans), BF16),
            pltpu.VMEM((rows, chans), BF16),
            pltpu.VMEM((rows, chans), BF16),
            pltpu.VMEM((4, chans, chans), BF16),
            pltpu.VMEM((rows, chans), BF16),
            pltpu.VMEM((rows, chans), BF16),
            pltpu.VMEM((rows, chans), F32),
            pltpu.VMEM((chans, 2 * SUB), BF16),
            pltpu.VMEM((SUB, chans), BF16),
            pltpu.VMEM((SUB, chans), BF16),
            pltpu.VMEM((groups, 2 * SUB), F32),
            pltpu.VMEM((groups // 2, SUB, 2 * SUB), BF16),
            pltpu.VMEM((subs, MODES, chans), F32),
            pltpu.VMEM((MODES, tile, LANES), F32),
            pltpu.VMEM((per_line, own, tile, LANES), F32),
            pltpu.VMEM((per_line, own, tile, LANES), F32),
            pltpu.VMEM((own, tile, LANES), F32),
            pltpu.VMEM((lines, own, tile, LANES), F32),
            pltpu.VMEM((per_line, own, tile, LANES), F32),
            pltpu.VMEM((per_line, own, tile, LANES), F32),
            pltpu.VMEM((2, subs, SUB, half), BF16),
            pltpu.VMEM((2, subs, SUB, half), BF16),
            pltpu.VMEM((2, 2, subs, SUB, half), BF16),
            pltpu.VMEM((2, 2, subs, SUB, half), BF16),
            dma((7,)),
            dma((subs,)),
            dma((per_line,)),
            dma((per_line,)),
            dma((lines,)),
            dma((lines,)),
            dma((per_line,)),
            dma((per_line,)),
            dma((2, subs)),
            dma((2, subs)),
            dma((2, 2, subs)),
            dma((2, 2, subs)),
        ],
        compiler_params=pltpu.CompilerParams(
            collective_id=0, has_side_effects=True, vmem_limit_bytes=56 * 1024 * 1024
        ),
    )(query, key_in, value, out_weight, rates.T, residues.T, skip_gain[None, :])


def solution(mesh):
    in_specs = (
        P("ctx", "tp"),
        P("ctx", "tp"),
        P("ctx", "tp"),
        P("tp", None),
        P("tp", None),
        P("tp"),
        P("tp", None),
    )
    lines = max(1, mesh.shape["ctx"] // MODES)
    return jax.shard_map(
        functools.partial(shards, lines),
        mesh=mesh,
        in_specs=in_specs,
        out_specs=P("ctx", "tp"),
        check_vma=False,
    )
```

time: 223 us -> 66.5 us (0.30)
  waiting for transfers between devices: 89.8 us -> 0 us
  local copies, waits for them, and re-layouts: 72.9 us -> 2.26 us
  Pallas kernels: 0 us -> 64.1 us
  matrix products: 38 us -> 0 us
  between operations: 13.6 us -> 0.01 us
  other arithmetic: 8.14 us -> 0 us
    reduce_scatter x1 -> x0, waiting for transfers between devices: 80 us -> none  [shards(): lax.psum_scatter(lax.dot_general(out_weight, mixed, (((0,), (0,)), ((), (...]
    pallas_call x0 -> x1, Pallas kernels: none -> 64.1 us  [shards(): pl.pallas_call(functools.partial(kernel, lines), name='hyena', out_shape=...]
    gather x2 -> x0, local copies, waits for them, and re-layouts: 61.8 us -> none  [shards(): jnp.take(filter_local, jnp.clip(lag_index, 0, SUB - 1), axis=1)]
    dot_general x4 -> x0, matrix products: 38 us -> none  [the longest x1 12.3 us: shards(): jnp.einsum('mct,mcj->cjt', decay_out, start_states, precision=lax.Precisi...]
    all_gather x1 -> x0, waiting for transfers between devices: 9.76 us -> none  [shards(): piece = lax.all_gather(summary[None], 'ctx', axis=0, tiled=True)]
    reduce_sum x2 -> x0, other arithmetic: 3.48 us -> none  [the longest x1 3.13 us: shards(): state = jnp.sum(weight * piece, axis=0)]
    convert_element_type x2 -> x0, other arithmetic: 2.73 us -> none  [the longest x1 2.72 us: shards(): return summed.T.astype(jnp.bfloat16)]
  transfers between devices with their start and end apart: 2 -> 0, of which waited for: 2 -> 0; matrix products, arithmetic and copies ran while one was open for 33% -> 0% of each run, Pallas kernels for 0% -> 0%
where the time goes in v1:
time: 66.5 us; the launch traced here: 66.3 us
  Pallas kernels  64.1 us (96%)
  local copies, waits for them, and re-layouts  2.26 us (3%)
    pallas_call x1, Pallas kernels, shards(): pl.pallas_call(functools.partial(kernel, lines), name='hyena', out_shape=...  64.1 us
    unnamed x1, local copies, waits for them, and re-layouts  2.26 us

profile of v1, /device:TPU:1, one launch (start us, length us, event | category | flops | bytes accessed | tf_op | source)
XLA Modules:
  0.0 66.3 jit_solution(14572132012168742536)
XLA Ops:
  0.0 64.1 %hyena.1 = bf16[512,1024]{1,0:T(8,128)(2,1)} custom-call(bf16[512,1024]{1,0:T(8,128)(2,1)} %q_hbm.1, bf16[512,1024]{1,0:T(8,128)(2,1)} %k_hbm.1, bf16[512,1024]{1,0:T(8,128)(2,1)} %v_hbm.1, bf16[1024,4096]{1,0:T(8,128)(2,1)} %w_hbm.1, f32[16,64]{1,0:T(8,128)} %bitcast.3, f32[16,64]{1,0:T(8,128)} %bitcast.4, f32[1,1024]{1,0:T(1,128)} %bitcast.5), custom_call_target="tpu_custom_call" | custom-call | tf_op jit(solution)/shard_map/hyena/pallas_call | solution.py:389
  64.1 2.3 %copy.9 = bf16[512,1024]{1,0:T(8,128)(2,1)} copy(bf16[512,1024]{1,0:T(8,128)(2,1)} %hyena.1) | data formatting | bytes 2097152

commit v2 on v1

--- a/solution.py
+++ b/solution.py
@@ -35,13 +35,12 @@
     rates_ref,
     residues_ref,
     skip_ref,
-    o_hbm,
+    ob,
     qb,
     kb,
     vb,
     ub,
     wb,
-    ob,
     mixed,
     local,
     d_tab,
@@ -62,7 +61,6 @@
     near_s,
     near_r,
     lsem,
-    osem,
     s_ss,
     s_rs,
     l_ss,
@@ -87,6 +85,8 @@
     right, left = lax.rem(tp + 1, 4), lax.rem(tp + 3, 4)
     sides = ((ctx, right), (ctx, left))
 
+    order = sorted(range(1, per_line), key=lambda k: abs(2 * k - per_line))
+
     def peer_j(k):
         return lax.rem(mj + k, per_line)
 
@@ -116,10 +116,8 @@
         w_loads[r] = pltpu.make_async_copy(
             w_hbm.at[:, pl.ds(start, chans)], wb.at[r], lsem.at[3 + r]
         )
-    for load in loads:
-        load.start()
-    for load in w_loads.values():
-        load.start()
+    loads[0].start()
+    loads[1].start()
 
     rates, residues = rates_ref[...].T, residues_ref[...].T
     pick = lax.broadcasted_iota(jnp.int32, (chans, MODES), 1) == (
@@ -152,6 +150,9 @@
 
     loads[0].wait()
     loads[1].wait()
+    loads[2].start()
+    for load in w_loads.values():
+        load.start()
     for j in range(subs):
         at = pl.ds(j * SUB, SUB)
         for b in range(blocks):
@@ -204,7 +205,7 @@
             device_id_type=MESH,
         )
 
-    for k in range(1, per_line):
+    for k in order:
         s_copy(k).start()
     s_recv[mj] = s_send[mj]
 
@@ -221,15 +222,21 @@
 
     lax.fori_loop(0, groups // 2, build, 0)
 
+    my_rate = rate3[pl.ds(mj * own, own)]
+    block_decay = jnp.exp(-my_rate * rows)
+    weights = []
+    for other in range(lines):
+        distance = mx - 1 - other
+        span = jnp.maximum(distance, 0) * (per_line * rows)
+        weights.append(jnp.where(distance >= 0, jnp.exp(-my_rate * span.astype(F32)), 0.0))
     for k in range(1, per_line):
         s_copy(k).wait_recv()
-    my_rate = rate3[pl.ds(mj * own, own)]
-    block_decay = jnp.exp(-my_rate * rows)
     total = jnp.zeros_like(my_rate)
     for j in range(per_line):
         x_send[j] = total
         total = block_decay * total + s_recv[j]
     l_send[...] = total
+    l_recv[mx] = total
     for k in range(1, lines):
         l_copy(k).start()
 
@@ -255,13 +262,11 @@
         l_copy(k).wait_recv()
     entering = jnp.zeros_like(total)
     for other in range(lines):
-        distance = mx - 1 - other
-        weight = jnp.exp(-my_rate * (jnp.maximum(distance, 0) * (per_line * rows)).astype(F32))
-        entering += jnp.where(distance >= 0, weight * l_recv[other], 0.0)
+        entering += weights[other] * l_recv[other]
     for j in range(per_line):
         x_send[j] = x_send[j] + entering
         entering = entering * block_decay
-    for k in range(1, per_line):
+    for k in order:
         x_copy(k).start()
     x_recv[mj] = x_send[mj]
 
@@ -342,10 +347,6 @@
     lax.fori_loop(0, subs, joint_step, 0)
     w_loads[0].wait()
 
-    def out_copy(j):
-        at = pl.ds(pl.multiple_of(j * SUB, SUB), SUB)
-        return pltpu.make_async_copy(ob.at[at], o_hbm.at[at], osem.at[j])
-
     def last_step(j, carry):
         at = pl.ds(pl.multiple_of(j * SUB, SUB), SUB)
         for part in range(2):
@@ -354,7 +355,6 @@
             near_copy(1, part, j).wait_recv()
             mine += near_r[0, part, j].astype(F32) + near_r[1, part, j].astype(F32)
             ob[at, part * half : (part + 1) * half] = mine.astype(BF16)
-        out_copy(j).start()
         return carry
 
     lax.fori_loop(0, subs, last_step, 0)
@@ -364,7 +364,6 @@
             far_copy(way, j).wait_send()
             for part in range(2):
                 near_copy(way, part, j).wait_send()
-        out_copy(j).wait()
         return carry
 
     lax.fori_loop(0, subs, drain, 0)
@@ -389,16 +388,15 @@
     return pl.pallas_call(
         functools.partial(kernel, lines),
         name="hyena",
-        out_shape=jax.ShapeDtypeStruct((rows, chans), BF16),
+        out_shape=pltpu.VMEM((rows, chans), BF16),
         in_specs=[hbm, hbm, hbm, hbm, vmem, vmem, vmem],
-        out_specs=hbm,
+        out_specs=vmem,
         scratch_shapes=[
             pltpu.VMEM((rows, chans), BF16),
             pltpu.VMEM((rows, chans), BF16),
             pltpu.VMEM((rows, chans), BF16),
             pltpu.VMEM((rows, chans), BF16),
             pltpu.VMEM((4, chans, chans), BF16),
-            pltpu.VMEM((rows, chans), BF16),
             pltpu.VMEM((rows, chans), BF16),
             pltpu.VMEM((rows, chans), F32),
             pltpu.VMEM((chans, 2 * SUB), BF16),
@@ -419,7 +417,6 @@
             pltpu.VMEM((2, 2, subs, SUB, half), BF16),
             pltpu.VMEM((2, 2, subs, SUB, half), BF16),
             dma((7,)),
-            dma((subs,)),
             dma((per_line,)),
             dma((per_line,)),
             dma((lines,)),

time: 66.5 us -> 63.8 us (0.959)
  Pallas kernels: 64.1 us -> 62.6 us
  local copies, waits for them, and re-layouts: 2.26 us -> 0.97 us
    pallas_call x1, Pallas kernels: 64.1 us -> 62.6 us  [shards(): pl.pallas_call(functools.partial(kernel, lines), name='hyena', out_shape=...]
    unnamed x1, local copies, waits for them, and re-layouts: 2.26 us -> 0.97 us
where the time goes in v2:
time: 63.8 us; the launch traced here: 63.6 us
  Pallas kernels  62.6 us (98%)
  local copies, waits for them, and re-layouts  0.97 us (2%)
    pallas_call x1, Pallas kernels, shards(): pl.pallas_call(functools.partial(kernel, lines), name='hyena', out_shape=...  62.6 us

profile of v2, /device:TPU:1, one launch (start us, length us, event | category | flops | bytes accessed | tf_op | source)
XLA Modules:
  0.0 63.6 jit_solution(11887666075040017235)
XLA Ops:
  0.0 62.6 %hyena.1 = bf16[512,1024]{1,0:T(8,128)(2,1)S(1)} custom-call(bf16[512,1024]{1,0:T(8,128)(2,1)} %q_hbm.1, bf16[512,1024]{1,0:T(8,128)(2,1)} %k_hbm.1, bf16[512,1024]{1,0:T(8,128)(2,1)} %v_hbm.1, bf16[1024,4096]{1,0:T(8,128)(2,1)} %w_hbm.1, f32[16,64]{1,0:T(8,128)} %bitcast.3, f32[16,64]{1,0:T(8,128)} %bitcast.4, f32[1,1024]{1,0:T(1,128)} %bitcast.5), custom_call_target="tpu_custom_call" | custom-call | tf_op jit(solution)/shard_map/hyena/pallas_call | solution.py:388
  62.6 1.0 %copy.9 = bf16[512,1024]{1,0:T(8,128)(2,1)} copy(bf16[512,1024]{1,0:T(8,128)(2,1)S(1)} %hyena.1) | data formatting | bytes 2097152

commit v3 on v2

--- a/solution.py
+++ b/solution.py
@@ -12,6 +12,7 @@
 SUB = 128
 LANES = 128
 BLK = 256
+STEP = 64
 MESH = pl.DeviceIdType.MESH
 F32 = jnp.float32
 BF16 = jnp.bfloat16
@@ -60,6 +61,10 @@
     far_r,
     near_s,
     near_r,
+    wp,
+    pair_r,
+    sum_s,
+    sum_r,
     lsem,
     s_ss,
     s_rs,
@@ -71,6 +76,18 @@
     far_rs,
     near_ss,
     near_rs,
+    wy_ss,
+    wy_rs,
+    wx_ss,
+    wx_rs,
+    wf_ss,
+    wf_rs,
+    sib_ss,
+    sib_rs,
+    pair_ss,
+    pair_rs,
+    sum_ss,
+    sum_rs,
 ):
     rows, chans = ub.shape
     subs = rows // SUB
@@ -84,6 +101,15 @@
     mx, mj = lax.div(ctx, per_line), lax.rem(ctx, per_line)
     right, left = lax.rem(tp + 1, 4), lax.rem(tp + 3, 4)
     sides = ((ctx, right), (ctx, left))
+    odd = lax.rem(tp, 2)
+    pair, opp = tp + 1 - 2 * odd, 3 - tp
+    way_pair, way_opp = odd, 1 - odd
+    core = lax.rem(ctx, 2)
+    sibling = ctx + 1 - 2 * core
+    slice_rows, piece_rows = chans // 8, chans // 16
+    pieces = 4
+    steps = pair_r.shape[0]
+    step_rows = pair_r.shape[1]
 
     order = sorted(range(1, per_line), key=lambda k: abs(2 * k - per_line))
 
@@ -205,8 +231,80 @@
             device_id_type=MESH,
         )
 
+    def piece(k, slot, lead, size):
+        start = core * (chans // 2) + slot * slice_rows + (k % 2) * piece_rows + lead
+        return pl.ds(pl.multiple_of(start, piece_rows // 2), size)
+
+    def wy_copy(k):
+        block = 1 - k // 2
+        column = pair if block == 0 else 3 - pair
+        at = piece(k, mx, 0, piece_rows)
+        return pltpu.make_async_remote_copy(
+            src_ref=w_hbm.at[at, pl.ds(pl.multiple_of(column * chans, chans), chans)],
+            dst_ref=wp.at[block, at],
+            send_sem=wy_ss.at[k],
+            recv_sem=wy_rs.at[k],
+            device_id=(ctx, pair),
+            device_id_type=MESH,
+        )
+
+    def x_side(way):
+        return (peer_x(1 if way == 0 else lines - 1) * per_line + mj, tp)
+
+    def wx_copy(k, way):
+        ref = wp.at[1 - k // 2, piece(k, mx, 0, piece_rows)]
+        return pltpu.make_async_remote_copy(
+            src_ref=ref,
+            dst_ref=ref,
+            send_sem=wx_ss.at[k, way],
+            recv_sem=wx_rs.at[k, way],
+            device_id=x_side(way),
+            device_id_type=MESH,
+        )
+
+    def wf_copy(k, way):
+        slot = peer_x(lines - 1 if way == 0 else 1)
+        ref = wp.at[1 - k // 2, piece(k, slot, way * (piece_rows // 2), piece_rows // 2)]
+        return pltpu.make_async_remote_copy(
+            src_ref=ref,
+            dst_ref=ref,
+            send_sem=wf_ss.at[k, way],
+            recv_sem=wf_rs.at[k, way],
+            device_id=x_side(way),
+            device_id_type=MESH,
+        )
+
+    def sib_copy(block):
+        ref = wp.at[block, pl.ds(pl.multiple_of(core * (chans // 2), chans // 2), chans // 2)]
+        return pltpu.make_async_remote_copy(
+            src_ref=ref,
+            dst_ref=ref,
+            send_sem=sib_ss.at[block],
+            recv_sem=sib_rs.at[block],
+            device_id=(sibling, tp),
+            device_id_type=MESH,
+        )
+
+    def spread_piece(k):
+        wy_copy(k).wait_recv()
+        for way in range(2):
+            wx_copy(k, way).start()
+
+    def pass_piece(k):
+        for way in range(2):
+            wx_copy(k, way).wait_recv()
+            wf_copy(k, way).start()
+
+    def share_block(block):
+        for k in (2 - 2 * block, 3 - 2 * block):
+            for way in range(2):
+                wf_copy(k, way).wait_recv()
+        sib_copy(block).start()
+
     for k in order:
         s_copy(k).start()
+    for k in range(pieces):
+        wy_copy(k).start()
     s_recv[mj] = s_send[mj]
 
     taps = jnp.sum((decay_in * residue_col).reshape(groups, MODES, SUB), axis=1)
@@ -239,6 +337,7 @@
     l_recv[mx] = total
     for k in range(1, lines):
         l_copy(k).start()
+    spread_piece(0)
 
     def inside(n, carry):
         j, b = lax.div(n, blocks), lax.rem(n, blocks)
@@ -257,6 +356,7 @@
 
     first_part = subs * blocks // 2
     lax.fori_loop(0, first_part, inside, 0)
+    spread_piece(1)
 
     for k in range(1, lines):
         l_copy(k).wait_recv()
@@ -274,33 +374,62 @@
     a_hi[...] = high
     a_lo[...] = low
     lax.fori_loop(first_part, subs * blocks, inside, 0)
+    pass_piece(0)
+    pass_piece(1)
+    spread_piece(2)
     loads[2].wait()
     for k in range(1, per_line):
         x_copy(k).wait_recv()
 
-    def far_copy(way, j):
-        return pltpu.make_async_remote_copy(
-            src_ref=far_s.at[way, j],
-            dst_ref=far_r.at[way, j],
-            send_sem=far_ss.at[way, j],
-            recv_sem=far_rs.at[way, j],
-            device_id=sides[way],
-            device_id_type=MESH,
-        )
-
-    def near_copy(way, part, j):
-        return pltpu.make_async_remote_copy(
-            src_ref=near_s.at[way, part, j],
-            dst_ref=near_r.at[way, part, j],
-            send_sem=near_ss.at[way, part, j],
-            recv_sem=near_rs.at[way, part, j],
-            device_id=sides[way],
-            device_id_type=MESH,
-        )
-
-    def project(j, r, part):
-        at = pl.ds(pl.multiple_of(j * SUB, SUB), SUB)
-        return dot(mixed[at, :], wb[r, :, part * half : (part + 1) * half])
+    def side_of(way):
+        return (ctx, lax.rem(tp + 1 + 2 * way, 4))
+
+    def far_copy(way):
+        return pltpu.make_async_remote_copy(
+            src_ref=far_s.at[way],
+            dst_ref=far_r.at[way],
+            send_sem=far_ss.at[way],
+            recv_sem=far_rs.at[way],
+            device_id=side_of(way),
+            device_id_type=MESH,
+        )
+
+    def near_copy(way, part):
+        return pltpu.make_async_remote_copy(
+            src_ref=near_s.at[way, part],
+            dst_ref=near_r.at[way, part],
+            send_sem=near_ss.at[way, part],
+            recv_sem=near_rs.at[way, part],
+            device_id=side_of(way),
+            device_id_type=MESH,
+        )
+
+    def tokens(h):
+        return pl.ds(pl.multiple_of(SUB + h * step_rows, step_rows), step_rows)
+
+    def pair_copy(h):
+        return pltpu.make_async_remote_copy(
+            src_ref=mixed.at[tokens(h)],
+            dst_ref=pair_r.at[h],
+            send_sem=pair_ss.at[h],
+            recv_sem=pair_rs.at[h],
+            device_id=(ctx, pair),
+            device_id_type=MESH,
+        )
+
+    def sum_copy(h):
+        return pltpu.make_async_remote_copy(
+            src_ref=sum_s.at[h],
+            dst_ref=sum_r.at[h],
+            send_sem=sum_ss.at[h],
+            recv_sem=sum_rs.at[h],
+            device_id=(ctx, opp),
+            device_id_type=MESH,
+        )
+
+    def project(r, part):
+        cols = pl.ds(pl.multiple_of(part * half, half), half)
+        return dot(mixed[:SUB, :], wb[r, :, cols])
 
     w_loads[2].wait()
     entry = jnp.concatenate(
@@ -308,9 +437,9 @@
     )
     diag_bf = diag.astype(BF16)
 
-    def far_step(j, carry):
+    def mix(j):
         at = pl.ds(pl.multiple_of(j * SUB, SUB), SUB)
-        start = jnp.exp(-rate_row * (j * SUB).astype(F32)) * entry + sums[j]
+        start = jnp.exp(-rate_row * (j * SUB * 1.0)) * entry + sums[j]
         x_hi, x_lo = split(start)
         for b in range(blocks):
             cols = slice(b * BLK, (b + 1) * BLK)
@@ -319,54 +448,97 @@
             past = dot(a_hi[:, cols], wide_hi) + dot(a_lo[:, cols], wide_hi)
             past += dot(a_hi[:, cols], wide_lo)
             mixed[at, cols] = (qb[at, cols].astype(F32) * (local[at, cols] + past)).astype(BF16)
-        for way in range(2):
-            far_s[way, j] = project(j, 2, way).astype(BF16)
-            far_copy(way, j).start()
-        return carry
-
-    lax.fori_loop(0, subs, far_step, 0)
+
+    per_sub = SUB // step_rows
+
+    def mix_and_send(j):
+        mix(j)
+        for h in range((j - 1) * per_sub, j * per_sub):
+            pair_copy(h).start()
+
+    def direct(way):
+        near_s[way, 1 - way] = project(1 + 2 * way, 1 - way).astype(BF16)
+        near_copy(way, 1 - way).start()
+
+    def joint(way):
+        part = project(1 + 2 * way, way)
+        far_copy(way).wait_recv()
+        near_s[way, way] = (part + far_r[way].astype(F32)).astype(BF16)
+        near_copy(way, way).start()
+
+    mix(0)
+    for way in range(2):
+        far_s[way] = project(2, way).astype(BF16)
+        far_copy(way).start()
+    mix_and_send(1)
     w_loads[1].wait()
     w_loads[3].wait()
-
-    def direct_step(j, carry):
-        for way in range(2):
-            near_s[way, 1 - way, j] = project(j, 1 + 2 * way, 1 - way).astype(BF16)
-            near_copy(way, 1 - way, j).start()
+    direct(way_opp)
+    for j in range(2, subs):
+        mix_and_send(j)
+    spread_piece(3)
+    joint(way_opp)
+    share_block(1)
+    direct(way_pair)
+    joint(way_pair)
+    pass_piece(2)
+    pass_piece(3)
+    w_loads[0].wait()
+    for part in range(2):
+        cols = slice(part * half, (part + 1) * half)
+        local[:SUB, cols] = project(0, part)
+
+    opp_slot = 3 - 2 * odd
+    sib_copy(1).wait_recv()
+
+    def sum_step(h, carry):
+        pair_copy(h).wait_recv()
+        mine, theirs = mixed[tokens(h), :], pair_r[h]
+        for part in range(2):
+            cols = slice(part * half, (part + 1) * half)
+            both = dot(mine, wb[opp_slot, :, cols]) + dot(theirs, wp[1, :, cols])
+            sum_s[h, :, cols] = both.astype(BF16)
+        sum_copy(h).start()
         return carry
 
-    lax.fori_loop(0, subs, direct_step, 0)
-
-    def joint_step(j, carry):
-        for way in range(2):
-            part = project(j, 1 + 2 * way, way)
-            far_copy(way, j).wait_recv()
-            near_s[way, way, j] = (part + far_r[way, j].astype(F32)).astype(BF16)
-            near_copy(way, way, j).start()
+    def own_step(h, carry):
+        mine, theirs = mixed[tokens(h), :], pair_r[h]
+        for part in range(2):
+            cols = slice(part * half, (part + 1) * half)
+            both = dot(mine, wb[0, :, cols]) + dot(theirs, wp[0, :, cols])
+            if part == 0:
+                sum_copy(h).wait_recv()
+            ob[tokens(h), cols] = (both + sum_r[h, :, cols].astype(F32)).astype(BF16)
         return carry
 
-    lax.fori_loop(0, subs, joint_step, 0)
-    w_loads[0].wait()
-
-    def last_step(j, carry):
-        at = pl.ds(pl.multiple_of(j * SUB, SUB), SUB)
+    def both_step(h, carry):
+        return own_step(h - 2, sum_step(h, carry))
+
+    lax.fori_loop(0, 2, sum_step, 0)
+    share_block(0)
+    sib_copy(0).wait_recv()
+    lax.fori_loop(2, steps, both_step, 0)
+    lax.fori_loop(steps - 2, steps, own_step, 0)
+    for part in range(2):
+        cols = slice(part * half, (part + 1) * half)
+        near_copy(0, part).wait_recv()
+        near_copy(1, part).wait_recv()
+        total = local[:SUB, cols] + near_r[0, part].astype(F32) + near_r[1, part].astype(F32)
+        ob[:SUB, cols] = total.astype(BF16)
+
+    for way in range(2):
+        far_copy(way).wait_send()
         for part in range(2):
-            mine = project(j, 0, part)
-            near_copy(0, part, j).wait_recv()
-            near_copy(1, part, j).wait_recv()
-            mine += near_r[0, part, j].astype(F32) + near_r[1, part, j].astype(F32)
-            ob[at, part * half : (part + 1) * half] = mine.astype(BF16)
-        return carry
-
-    lax.fori_loop(0, subs, last_step, 0)
-
-    def drain(j, carry):
-        for way in range(2):
-            far_copy(way, j).wait_send()
-            for part in range(2):
-                near_copy(way, part, j).wait_send()
-        return carry
-
-    lax.fori_loop(0, subs, drain, 0)
+            near_copy(way, part).wait_send()
+        for k in range(pieces):
+            wx_copy(k, way).wait_send()
+            wf_copy(k, way).wait_send()
+        sib_copy(way).wait_send()
+    for k in range(pieces):
+        wy_copy(k).wait_send()
+    for h in range(steps):
+        pair_copy(h).wait_send()
+        sum_copy(h).wait_send()
     for k in range(1, per_line):
         s_copy(k).wait_send()
         x_copy(k).wait_send()
@@ -378,6 +550,7 @@
     rows, chans = query.shape
     groups = chans // GROUP
     subs = rows // SUB
+    steps = (rows - SUB) // STEP
     half = chans // 2
     per_line = lax.axis_size("ctx") // lines
     own = MODES // per_line
@@ -412,10 +585,14 @@
             pltpu.VMEM((lines, own, tile, LANES), F32),
             pltpu.VMEM((per_line, own, tile, LANES), F32),
             pltpu.VMEM((per_line, own, tile, LANES), F32),
-            pltpu.VMEM((2, subs, SUB, half), BF16),
-            pltpu.VMEM((2, subs, SUB, half), BF16),
-            pltpu.VMEM((2, 2, subs, SUB, half), BF16),
-            pltpu.VMEM((2, 2, subs, SUB, half), BF16),
+            pltpu.VMEM((2, SUB, half), BF16),
+            pltpu.VMEM((2, SUB, half), BF16),
+            pltpu.VMEM((2, 2, SUB, half), BF16),
+            pltpu.VMEM((2, 2, SUB, half), BF16),
+            pltpu.VMEM((2, chans, chans), BF16),
+            pltpu.VMEM((steps, STEP, chans), BF16),
+            pltpu.VMEM((steps, STEP, chans), BF16),
+            pltpu.VMEM((steps, STEP, chans), BF16),
             dma((7,)),
             dma((per_line,)),
             dma((per_line,)),
@@ -423,10 +600,22 @@
             dma((lines,)),
             dma((per_line,)),
             dma((per_line,)),
-            dma((2, subs)),
-            dma((2, subs)),
-            dma((2, 2, subs)),
-            dma((2, 2, subs)),
+            dma((2,)),
+            dma((2,)),
+            dma((2, 2)),
+            dma((2, 2)),
+            dma((4,)),
+            dma((4,)),
+            dma((4, 2)),
+            dma((4, 2)),
+            dma((4, 2)),
+            dma((4, 2)),
+            dma((2,)),
+            dma((2,)),
+            dma((steps,)),
+            dma((steps,)),
+            dma((steps,)),
+            dma((steps,)),
         ],
         compiler_params=pltpu.CompilerParams(
             collective_id=0, has_side_effects=True, vmem_limit_bytes=56 * 1024 * 1024

time: 63.8 us -> 57.7 us (0.904)
  Pallas kernels: 62.6 us -> 56.6 us
    pallas_call x1, Pallas kernels: 62.6 us -> 56.6 us  [shards(): pl.pallas_call(functools.partial(kernel, lines), name='hyena', out_shape=...]
where the time goes in v3:
time: 57.7 us; the launch traced here: 57.5 us
  Pallas kernels  56.6 us (98%)
  local copies, waits for them, and re-layouts  0.97 us (2%)
    pallas_call x1, Pallas kernels, shards(): pl.pallas_call(functools.partial(kernel, lines), name='hyena', out_shape=...  56.6 us

profile of v3, /device:TPU:1, one launch (start us, length us, event | category | flops | bytes accessed | tf_op | source)
XLA Modules:
  0.0 57.5 jit_solution(10812692687481183387)
XLA Ops:
  0.0 56.6 %hyena.1 = bf16[512,1024]{1,0:T(8,128)(2,1)S(1)} custom-call(bf16[512,1024]{1,0:T(8,128)(2,1)} %q_hbm.1, bf16[512,1024]{1,0:T(8,128)(2,1)} %k_hbm.1, bf16[512,1024]{1,0:T(8,128)(2,1)} %v_hbm.1, bf16[1024,4096]{1,0:T(8,128)(2,1)} %w_hbm.1, f32[16,64]{1,0:T(8,128)} %bitcast.3, f32[16,64]{1,0:T(8,128)} %bitcast.4, f32[1,1024]{1,0:T(1,128)} %bitcast.5), custom_call_target="tpu_custom_call" | custom-call | tf_op jit(solution)/shard_map/hyena/pallas_call | solution.py:561
  56.6 1.0 %copy.9 = bf16[512,1024]{1,0:T(8,128)(2,1)} copy(bf16[512,1024]{1,0:T(8,128)(2,1)S(1)} %hyena.1) | data formatting | bytes 2097152

commit v4 on v3

--- a/solution.py
+++ b/solution.py
@@ -108,8 +108,8 @@
     sibling = ctx + 1 - 2 * core
     slice_rows, piece_rows = chans // 8, chans // 16
     pieces = 4
-    steps = pair_r.shape[0]
-    step_rows = pair_r.shape[1]
+    step_rows = STEP
+    steps = (rows - SUB) // step_rows
 
     order = sorted(range(1, per_line), key=lambda k: abs(2 * k - per_line))
 
@@ -375,8 +375,8 @@
     a_lo[...] = low
     lax.fori_loop(first_part, subs * blocks, inside, 0)
     pass_piece(0)
+    spread_piece(2)
     pass_piece(1)
-    spread_piece(2)
     loads[2].wait()
     for k in range(1, per_line):
         x_copy(k).wait_recv()
@@ -404,13 +404,13 @@
             device_id_type=MESH,
         )
 
-    def tokens(h):
-        return pl.ds(pl.multiple_of(SUB + h * step_rows, step_rows), step_rows)
+    def tokens(h, skip=SUB, size=step_rows):
+        return pl.ds(pl.multiple_of(skip + h * size, step_rows), size)
 
     def pair_copy(h):
         return pltpu.make_async_remote_copy(
             src_ref=mixed.at[tokens(h)],
-            dst_ref=pair_r.at[h],
+            dst_ref=pair_r.at[tokens(h, 0)],
             send_sem=pair_ss.at[h],
             recv_sem=pair_rs.at[h],
             device_id=(ctx, pair),
@@ -419,8 +419,8 @@
 
     def sum_copy(h):
         return pltpu.make_async_remote_copy(
-            src_ref=sum_s.at[h],
-            dst_ref=sum_r.at[h],
+            src_ref=sum_s.at[tokens(h, 0)],
+            dst_ref=sum_r.at[tokens(h, 0)],
             send_sem=sum_ss.at[h],
             recv_sem=sum_rs.at[h],
             device_id=(ctx, opp),
@@ -482,43 +482,50 @@
     direct(way_pair)
     joint(way_pair)
     pass_piece(2)
-    pass_piece(3)
     w_loads[0].wait()
     for part in range(2):
         cols = slice(part * half, (part + 1) * half)
         local[:SUB, cols] = project(0, part)
 
     opp_slot = 3 - 2 * odd
-    sib_copy(1).wait_recv()
-
-    def sum_step(h, carry):
+
+    def sum_step(h):
         pair_copy(h).wait_recv()
-        mine, theirs = mixed[tokens(h), :], pair_r[h]
+        mine, theirs = mixed[tokens(h), :], pair_r[tokens(h, 0), :]
         for part in range(2):
             cols = slice(part * half, (part + 1) * half)
             both = dot(mine, wb[opp_slot, :, cols]) + dot(theirs, wp[1, :, cols])
-            sum_s[h, :, cols] = both.astype(BF16)
+            sum_s[tokens(h, 0), cols] = both.astype(BF16)
         sum_copy(h).start()
-        return carry
-
-    def own_step(h, carry):
-        mine, theirs = mixed[tokens(h), :], pair_r[h]
+
+    def own_step(n):
+        at, off = tokens(n, SUB, SUB), tokens(n, 0, SUB)
+        mine, theirs = mixed[at, :], pair_r[off, :]
         for part in range(2):
             cols = slice(part * half, (part + 1) * half)
-            both = dot(mine, wb[0, :, cols]) + dot(theirs, wp[0, :, cols])
-            if part == 0:
-                sum_copy(h).wait_recv()
-            ob[tokens(h), cols] = (both + sum_r[h, :, cols].astype(F32)).astype(BF16)
-        return carry
-
-    def both_step(h, carry):
-        return own_step(h - 2, sum_step(h, carry))
-
-    lax.fori_loop(0, 2, sum_step, 0)
+            local[at, cols] = dot(mine, wb[0, :, cols]) + dot(theirs, wp[0, :, cols])
+
+    def finish(n):
+        for h in range(n * per_sub, (n + 1) * per_sub):
+            sum_copy(h).wait_recv()
+            ob[tokens(h), :] = (local[tokens(h), :] + sum_r[tokens(h, 0), :].astype(F32)).astype(BF16)
+
+    sib_copy(1).wait_recv()
+    sum_step(0)
+    pass_piece(3)
+    sum_step(1)
     share_block(0)
+    sum_step(2)
+    sum_step(3)
     sib_copy(0).wait_recv()
-    lax.fori_loop(2, steps, both_step, 0)
-    lax.fori_loop(steps - 2, steps, own_step, 0)
+    own_step(0)
+    sum_step(4)
+    sum_step(5)
+    finish(0)
+    own_step(1)
+    own_step(2)
+    finish(1)
+    finish(2)
     for part in range(2):
         cols = slice(part * half, (part + 1) * half)
         near_copy(0, part).wait_recv()
@@ -590,9 +597,9 @@
             pltpu.VMEM((2, 2, SUB, half), BF16),
             pltpu.VMEM((2, 2, SUB, half), BF16),
             pltpu.VMEM((2, chans, chans), BF16),
-            pltpu.VMEM((steps, STEP, chans), BF16),
-            pltpu.VMEM((steps, STEP, chans), BF16),
-            pltpu.VMEM((steps, STEP, chans), BF16),
+            pltpu.VMEM((rows - SUB, chans), BF16),
+            pltpu.VMEM((rows - SUB, chans), BF16),
+            pltpu.VMEM((rows - SUB, chans), BF16),
             dma((7,)),
             dma((per_line,)),
             dma((per_line,)),

time: 57.7 us -> 56.2 us (0.974)
  Pallas kernels: 56.6 us -> 55.1 us
    pallas_call x1, Pallas kernels: 56.6 us -> 55.1 us  [shards(): pl.pallas_call(functools.partial(kernel, lines), name='hyena', out_shape=...]
where the time goes in v4:
time: 56.2 us; the launch traced here: 56 us
  Pallas kernels  55.1 us (98%)
  local copies, waits for them, and re-layouts  0.97 us (2%)
    pallas_call x1, Pallas kernels, shards(): pl.pallas_call(functools.partial(kernel, lines), name='hyena', out_shape=...  55.1 us

profile of v4, /device:TPU:1, one launch (start us, length us, event | category | flops | bytes accessed | tf_op | source)
XLA Modules:
  0.0 56.0 jit_solution(5440671680481794403)
XLA Ops:
  0.0 55.1 %hyena.1 = bf16[512,1024]{1,0:T(8,128)(2,1)S(1)} custom-call(bf16[512,1024]{1,0:T(8,128)(2,1)} %q_hbm.1, bf16[512,1024]{1,0:T(8,128)(2,1)} %k_hbm.1, bf16[512,1024]{1,0:T(8,128)(2,1)} %v_hbm.1, bf16[1024,4096]{1,0:T(8,128)(2,1)} %w_hbm.1, f32[16,64]{1,0:T(8,128)} %bitcast.3, f32[16,64]{1,0:T(8,128)} %bitcast.4, f32[1,1024]{1,0:T(1,128)} %bitcast.5), custom_call_target="tpu_custom_call" | custom-call | tf_op jit(solution)/shard_map/hyena/pallas_call | solution.py:568
  55.1 1.0 %copy.9 = bf16[512,1024]{1,0:T(8,128)(2,1)} copy(bf16[512,1024]{1,0:T(8,128)(2,1)S(1)} %hyena.1) | data formatting | bytes 2097152

commit v5 on v4

--- a/solution.py
+++ b/solution.py
@@ -106,7 +106,7 @@
     way_pair, way_opp = odd, 1 - odd
     core = lax.rem(ctx, 2)
     sibling = ctx + 1 - 2 * core
-    slice_rows, piece_rows = chans // 8, chans // 16
+    piece_rows = chans // 16
     pieces = 4
     step_rows = STEP
     steps = (rows - SUB) // step_rows
@@ -232,7 +232,7 @@
         )
 
     def piece(k, slot, lead, size):
-        start = core * (chans // 2) + slot * slice_rows + (k % 2) * piece_rows + lead
+        start = core * (chans // 2) + (k % 2) * (chans // 4) + slot * piece_rows + lead
         return pl.ds(pl.multiple_of(start, piece_rows // 2), size)
 
     def wy_copy(k):
@@ -274,13 +274,14 @@
             device_id_type=MESH,
         )
 
-    def sib_copy(block):
-        ref = wp.at[block, pl.ds(pl.multiple_of(core * (chans // 2), chans // 2), chans // 2)]
+    def sib_copy(k):
+        start = core * (chans // 2) + (k % 2) * (chans // 4)
+        ref = wp.at[1 - k // 2, pl.ds(pl.multiple_of(start, chans // 4), chans // 4)]
         return pltpu.make_async_remote_copy(
             src_ref=ref,
             dst_ref=ref,
-            send_sem=sib_ss.at[block],
-            recv_sem=sib_rs.at[block],
+            send_sem=sib_ss.at[k],
+            recv_sem=sib_rs.at[k],
             device_id=(sibling, tp),
             device_id_type=MESH,
         )
@@ -295,11 +296,10 @@
             wx_copy(k, way).wait_recv()
             wf_copy(k, way).start()
 
-    def share_block(block):
-        for k in (2 - 2 * block, 3 - 2 * block):
-            for way in range(2):
-                wf_copy(k, way).wait_recv()
-        sib_copy(block).start()
+    def share_piece(k):
+        for way in range(2):
+            wf_copy(k, way).wait_recv()
+        sib_copy(k).start()
 
     for k in order:
         s_copy(k).start()
@@ -466,19 +466,23 @@
         near_s[way, way] = (part + far_r[way].astype(F32)).astype(BF16)
         near_copy(way, way).start()
 
-    mix(0)
-    for way in range(2):
+    def far(way):
         far_s[way] = project(2, way).astype(BF16)
         far_copy(way).start()
+
+    mix(0)
+    far(way_pair)
+    far(way_opp)
     mix_and_send(1)
     w_loads[1].wait()
     w_loads[3].wait()
     direct(way_opp)
+    share_piece(0)
     for j in range(2, subs):
         mix_and_send(j)
     spread_piece(3)
     joint(way_opp)
-    share_block(1)
+    share_piece(1)
     direct(way_pair)
     joint(way_pair)
     pass_piece(2)
@@ -510,14 +514,17 @@
             sum_copy(h).wait_recv()
             ob[tokens(h), :] = (local[tokens(h), :] + sum_r[tokens(h, 0), :].astype(F32)).astype(BF16)
 
+    sib_copy(0).wait_recv()
     sib_copy(1).wait_recv()
     sum_step(0)
     pass_piece(3)
+    share_piece(2)
     sum_step(1)
-    share_block(0)
+    share_piece(3)
     sum_step(2)
     sum_step(3)
-    sib_copy(0).wait_recv()
+    sib_copy(2).wait_recv()
+    sib_copy(3).wait_recv()
     own_step(0)
     sum_step(4)
     sum_step(5)
@@ -540,9 +547,9 @@
         for k in range(pieces):
             wx_copy(k, way).wait_send()
             wf_copy(k, way).wait_send()
-        sib_copy(way).wait_send()
     for k in range(pieces):
         wy_copy(k).wait_send()
+        sib_copy(k).wait_send()
     for h in range(steps):
         pair_copy(h).wait_send()
         sum_copy(h).wait_send()
@@ -617,8 +624,8 @@
             dma((4, 2)),
             dma((4, 2)),
             dma((4, 2)),
-            dma((2,)),
-            dma((2,)),
+            dma((4,)),
+            dma((4,)),
             dma((steps,)),
             dma((steps,)),
             dma((steps,)),

time: 56.2 us -> 54.9 us (0.977)
  Pallas kernels: 55.1 us -> 53.7 us
    pallas_call x1, Pallas kernels: 55.1 us -> 53.7 us  [shards(): pl.pallas_call(functools.partial(kernel, lines), name='hyena', out_shape=...]
where the time goes in v5:
time: 54.9 us; the launch traced here: 54.7 us
  Pallas kernels  53.7 us (98%)
  local copies, waits for them, and re-layouts  0.97 us (2%)
    pallas_call x1, Pallas kernels, shards(): pl.pallas_call(functools.partial(kernel, lines), name='hyena', out_shape=...  53.7 us

profile of v5, /device:TPU:1, one launch (start us, length us, event | category | flops | bytes accessed | tf_op | source)
XLA Modules:
  0.0 54.7 jit_solution(11901256530977867442)
XLA Ops:
  0.0 53.7 %hyena.1 = bf16[512,1024]{1,0:T(8,128)(2,1)S(1)} custom-call(bf16[512,1024]{1,0:T(8,128)(2,1)} %q_hbm.1, bf16[512,1024]{1,0:T(8,128)(2,1)} %k_hbm.1, bf16[512,1024]{1,0:T(8,128)(2,1)} %v_hbm.1, bf16[1024,4096]{1,0:T(8,128)(2,1)} %w_hbm.1, f32[16,64]{1,0:T(8,128)} %bitcast.3, f32[16,64]{1,0:T(8,128)} %bitcast.4, f32[1,1024]{1,0:T(1,128)} %bitcast.5), custom_call_target="tpu_custom_call" | custom-call | tf_op jit(solution)/shard_map/hyena/pallas_call | solution.py:575
  53.7 1.0 %copy.9 = bf16[512,1024]{1,0:T(8,128)(2,1)} copy(bf16[512,1024]{1,0:T(8,128)(2,1)S(1)} %hyena.1) | data formatting | bytes 2097152

commit v6 on v5

--- a/solution.py
+++ b/solution.py
@@ -481,8 +481,8 @@
     for j in range(2, subs):
         mix_and_send(j)
     spread_piece(3)
+    share_piece(1)
     joint(way_opp)
-    share_piece(1)
     direct(way_pair)
     joint(way_pair)
     pass_piece(2)

time: 54.9 us -> 54.9 us (level)
  no operation moved by 1% of the time
where the time goes in v6:
time: 54.9 us; the launch traced here: 54.7 us
  Pallas kernels  53.7 us (98%)
  local copies, waits for them, and re-layouts  0.97 us (2%)
    pallas_call x1, Pallas kernels, shards(): pl.pallas_call(functools.partial(kernel, lines), name='hyena', out_shape=...  53.7 us

profile of v6, /device:TPU:1, one launch (start us, length us, event | category | flops | bytes accessed | tf_op | source)
XLA Modules:
  0.0 54.7 jit_solution(8265549154497165645)
XLA Ops:
  0.0 53.7 %hyena.1 = bf16[512,1024]{1,0:T(8,128)(2,1)S(1)} custom-call(bf16[512,1024]{1,0:T(8,128)(2,1)} %q_hbm.1, bf16[512,1024]{1,0:T(8,128)(2,1)} %k_hbm.1, bf16[512,1024]{1,0:T(8,128)(2,1)} %v_hbm.1, bf16[1024,4096]{1,0:T(8,128)(2,1)} %w_hbm.1, f32[16,64]{1,0:T(8,128)} %bitcast.3, f32[16,64]{1,0:T(8,128)} %bitcast.4, f32[1,1024]{1,0:T(1,128)} %bitcast.5), custom_call_target="tpu_custom_call" | custom-call | tf_op jit(solution)/shard_map/hyena/pallas_call | solution.py:575
  53.7 1.0 %copy.9 = bf16[512,1024]{1,0:T(8,128)(2,1)} copy(bf16[512,1024]{1,0:T(8,128)(2,1)S(1)} %hyena.1) | data formatting | bytes 2097152
